TPU v7x, 32 devices: a whole 2x2x4 slice. The times are simulated.
32 devices in a mesh: row: 8 (over z, core), aux: 4 (over y, x).
Axes of the slice: x: 2, y: 2, z: 4, core: 2. Of those that a mesh axis runs over, the one named last changes fastest.
Arguments:
- factor_ia: float32 [64, 12288], P('row', 'aux'), may hold values from -0.8 to 0.8
- factor_jb: float32 [5120, 12288], P('row', 'aux'), may hold values from -0.8 to 0.8
- denominators: float32 [64, 5120], P(None, 'row'), may hold values from 0.5 to 8
Outputs:
- grad_jb: float32 [5120, 12288], P('row', 'aux')
- grad_ia: float32 [64, 12288], P('row', 'aux')
All inputs are finite; a program needn't handle non-finite values.
Results may differ from a plain program's by a relative error of at most 0.00011.
Values sent between devices are 32-bit elements; how exact they have to be, the bound alone decides.
No kernel may reach another device: no remote copies, remote signals or barrier semaphores. Data moves between devices by JAX's collectives and lax.ppermute only.
A program may use at most 64 MiB of HBM per device.

v0:
```python
import jax
import jax.numpy as jnp
from jax import lax
from jax.sharding import PartitionSpec as P


def per_device(factor_ia, factor_jb, denominators):
    whole_ia = lax.all_gather(factor_ia, "row", axis=0, tiled=True)
    partial_value = lax.dot_general(
        whole_ia,
        factor_jb,
        (((1,), (1,)), ((), ())),
        precision=lax.Precision.HIGHEST,
        preferred_element_type=jnp.float32,
    )
    share_width = denominators.shape[1] // lax.axis_size("aux")
    share_start = lax.axis_index("aux") * share_width
    integral_part = lax.psum_scatter(partial_value, "aux", scatter_dimension=1, tiled=True)
    denom_part = lax.dynamic_slice_in_dim(denominators, share_start, share_width, 1)
    amplitudes = lax.all_gather(integral_part / denom_part, "aux", axis=1, tiled=True)
    grad_jb = lax.dot_general(
        amplitudes,
        whole_ia,
        (((0,), (0,)), ((), ())),
        precision=lax.Precision.HIGHEST,
        preferred_element_type=jnp.float32,
    )
    grad_ia = lax.psum_scatter(
        jnp.dot(
            amplitudes,
            factor_jb,
            precision=lax.Precision.HIGHEST,
            preferred_element_type=jnp.float32,
        ),
        "row",
        scatter_dimension=0,
        tiled=True,
    )
    return (grad_jb, grad_ia)


def solution(mesh):
    return jax.shard_map(
        per_device,
        mesh=mesh,
        in_specs=(P("row", "aux"), P("row", "aux"), P(None, "row")),
        out_specs=(P("row", "aux"), P("row", "aux")),
        check_vma=False,
    )
```

profile of v0, /device:TPU:0, one launch (start us, length us, event | category | flops | bytes accessed | tf_op | source)
XLA Modules:
  0.0 119.1 jit_solution(13380019254326274909)
XLA Ops:
  7.2 0.0 reduce-scatter.7.cloned.1.call-start
  7.2 17.4 %all_gather.6 = f32[64,3072]{1,0:T(8,128)S(1)} all-gather(f32[8,3072]{1,0:T(8,128)} %param.3), channel_id=1, replica_groups=mesh['row'=8,'aux'=4] {'row'}, dimensions={0}, use_global_device_ids=true | all-gather | bytes 884736 | tf_op jit(solution)/shard_map/all_gather | solution.py:8
  24.6 9.2 %convolution_bitcast_fusion = f32[640,64]{1,0:T(8,128)} fusion(f32[64,3072]{1,0:T(8,128)S(1)} %all_gather.6, f32[640,3072]{1,0:T(8,128)} %param.4), kind=kOutput, calls=%fused_computation | convolution fusion | flops 1509949440 | bytes 8814592
  33.8 0.0 reduce-scatter.7.cloned.1.call-update
  33.8 0.0 reduce-scatter.5.cloned.1.call-start
  33.9 25.8 %reduce-scatter.7.cloned.1.call-done = f32[160,64]{1,0:T(8,128)} async-done(((f32[640,64]{1,0:T(8,128)}), f32[160,64]{1,0:T(8,128)}) %reduce-scatter.7.cloned.1.call-update) | async-done | bytes 40976
  59.7 1.0 copy.8
  60.6 1.0 divide_bitcast_fusion
  61.6 9.3 %all-gather = f32[4,160,64]{1,2,0:T(8,128)S(1)} all-gather(f32[1,160,64]{1,2,0:T(8,128)S(1)} %divide_bitcast_fusion), channel_id=1, replica_groups=mesh['row'=8,'aux'=4] {'aux'}, dimensions={0}, use_global_device_ids=true | all-gather | bytes 204800 | tf_op jit(solution)/shard_map/all_gather | solution.py:20
  70.9 0.2 copy.6
  71.1 0.2 reshape.5
  71.3 8.9 %fusion.1 = f32[64,3072]{1,0:T(8,128)} fusion(f32[640,64]{0,1:T(8,128)S(1)} %reshape.5, f32[640,3072]{1,0:T(8,128)} %param.4), kind=kOutput, calls=%fused_computation.3 | convolution fusion | flops 1509949440 | bytes 8814592 | tf_op jit(solution)/shard_map/dot_general | solution.py:29
  80.2 0.0 reduce-scatter.5.cloned.1.call-update
  80.2 8.5 %fusion = f32[640,3072]{1,0:T(8,128)} fusion(f32[640,64]{0,1:T(8,128)S(1)} %reshape.5, f32[64,3072]{1,0:T(8,128)S(1)} %all_gather.6), kind=kOutput, calls=%fused_computation.2 | convolution fusion | flops 1509949440 | bytes 8814592 | tf_op jit(solution)/shard_map/dot_general | solution.py:21
  88.7 23.5 %reduce-scatter.5.cloned.1.call-done = f32[8,3072]{1,0:T(8,128)} async-done(((f32[64,3072]{1,0:T(8,128)}), f32[8,3072]{1,0:T(8,128)}) %reduce-scatter.5.cloned.1.call-update) | async-done | bytes 98320 | tf_op jit(solution)/shard_map/reduce_scatter | solution.py:28
Async XLA Ops:
  7.2 52.5 %reduce-scatter.7.cloned.1.call-start = ((), (), s32[]{:S(2)}) async-start(), calls=%async_computation.3 | async-start | bytes 409600
  33.8 78.4 %reduce-scatter.5.cloned.1.call-start = ((), (), s32[]{:S(2)}) async-start(), calls=%async_computation.2 | async-start | bytes 884736 | tf_op jit(solution)/shard_map/reduce_scatter | solution.py:28
Sparse Core Ops, SparseCore 0:
  34.0 25.6 reduce-scatter.6
  80.4 31.8 reduce-scatter.4
where the time goes:
time: 119 us
  waiting for transfers between devices  49.3 us (41%)
  blocking collectives  26.7 us (22%)
  matrix products  26.6 us (22%)
  between operations  14.1 us (12%)
  local copies, waits for them, and re-layouts  1.31 us (1%)
    unnamed x3, waiting for transfers between devices  25.8 us
    reduce_scatter x1, waiting for transfers between devices, per_device(): lax.psum_scatter(jnp.dot(amplitudes, factor_jb, precision=lax.Precision.H...  23.5 us
    all_gather x1, blocking collectives, per_device(): whole_ia = lax.all_gather(factor_ia, 'row', axis=0, tiled=True)  17.4 us
    all_gather x1, blocking collectives, per_device(): lax.all_gather(integral_part / denom_part, 'aux', axis=1, tiled=True)  9.29 us
    unnamed x1, matrix products  9.18 us
    dot_general x1, matrix products, per_device(): jnp.dot(amplitudes, factor_jb, precision=lax.Precision.HIGHEST, preferred...  8.92 us
    dot_general x1, matrix products, per_device(): lax.dot_general(amplitudes, whole_ia, (((0,), (0,)), ((), ())), precision...  8.48 us
  transfers between devices with their start and end apart: 2, of which 2 were waited for; matrix products, arithmetic and copies ran while one was open for 7% of the time, Pallas kernels for 0%

commit v1 on v0

--- a/solution.py
+++ b/solution.py
@@ -5,7 +5,12 @@
 
 
 def per_device(factor_ia, factor_jb, denominators):
-    whole_ia = lax.all_gather(factor_ia, "row", axis=0, tiled=True)
+    ring = [factor_ia]
+    for hop in range(7):
+        ring.append(lax.ppermute(ring[-1], "row", [(dev, (dev + 1) % 8) for dev in range(8)]))
+    whole_ia = jnp.roll(
+        jnp.concatenate(ring[::-1], axis=0), (lax.axis_index("row") + 1) * ring[0].shape[0], axis=0
+    )
     partial_value = lax.dot_general(
         whole_ia,
         factor_jb,

time: 119 us -> 143 us (1.20)
  waiting for transfers between devices: 49.3 us -> 88.5 us
  blocking collectives: 26.7 us -> 9.45 us
    ppermute x0 -> x7, waiting for transfers between devices: none -> 41.6 us  [per_device(): lax.ppermute(ring[-1], 'row', [(dev, (dev + 1) % 8) for dev in range(8)])]
    all_gather x1 -> x0, blocking collectives: 17.4 us -> none  [per_device(): whole_ia = lax.all_gather(factor_ia, 'row', axis=0, tiled=True)]
    unnamed x3, waiting for transfers between devices: 25.8 us -> 23.4 us
  transfers between devices with their start and end apart: 2 -> 9, of which waited for: 2 -> 9; matrix products, arithmetic and copies ran while one was open for 7% -> 6% of each run, Pallas kernels for 0% -> 0%
where the time goes in v1:
time: 143 us
  waiting for transfers between devices  88.5 us (62%)
  matrix products  26.6 us (19%)
  between operations  14.2 us (10%)
  blocking collectives  9.45 us (7%)
  local copies, waits for them, and re-layouts  2.36 us (2%)
    ppermute x7, waiting for transfers between devices, per_device(): lax.ppermute(ring[-1], 'row', [(dev, (dev + 1) % 8) for dev in range(8)])  41.6 us
    reduce_scatter x1, waiting for transfers between devices, per_device(): lax.psum_scatter(jnp.dot(amplitudes, factor_jb, precision=lax.Precision.H...  23.6 us
    unnamed x3, waiting for transfers between devices  23.4 us
    all_gather x1, blocking collectives, per_device(): lax.all_gather(integral_part / denom_part, 'aux', axis=1, tiled=True)  9.45 us
    unnamed x1, matrix products  9.21 us
    dot_general x1, matrix products, per_device(): jnp.dot(amplitudes, factor_jb, precision=lax.Precision.HIGHEST, preferred...  8.92 us
    dot_general x1, matrix products, per_device(): lax.dot_general(amplitudes, whole_ia, (((0,), (0,)), ((), ())), precision...  8.49 us
  transfers between devices with their start and end apart: 9, of which 9 were waited for; matrix products, arithmetic and copies ran while one was open for 6% of the time, Pallas kernels for 0%

profile of v1, /device:TPU:0, one launch (start us, length us, event | category | flops | bytes accessed | tf_op | source)
XLA Modules:
  0.0 142.8 jit_solution(9023773519183549174)
XLA Ops:
  7.2 0.0 copy-start
  7.2 0.0 reduce-scatter.7.cloned.1.call-start
  7.2 0.5 collective-permute-start
  7.8 6.5 %collective-permute-done = f32[8,3072]{1,0:T(8,128)S(1)} collective-permute-done((f32[8,3072]{1,0:T(8,128)}, f32[8,3072]{1,0:T(8,128)S(1)}, u32[]{:S(2)}, u32[]{:S(2)}) %collective-permute-start) | collective-permute-done | bytes 98336 | tf_op jit(solution)/shard_map/ppermute | solution.py:10
  14.3 0.0 collective-permute-start.1
  14.3 5.8 %collective-permute-done.1 = f32[8,3072]{1,0:T(8,128)S(1)} collective-permute-done((f32[8,3072]{1,0:T(8,128)S(1)}, f32[8,3072]{1,0:T(8,128)S(1)}, u32[]{:S(2)}, u32[]{:S(2)}) %collective-permute-start.1) | collective-permute-done | bytes 98336 | tf_op jit(solution)/shard_map/ppermute | solution.py:10
  20.1 0.0 collective-permute-start.2
  20.1 5.8 %collective-permute-done.2 = f32[8,3072]{1,0:T(8,128)S(1)} collective-permute-done((f32[8,3072]{1,0:T(8,128)S(1)}, f32[8,3072]{1,0:T(8,128)S(1)}, u32[]{:S(2)}, u32[]{:S(2)}) %collective-permute-start.2) | collective-permute-done | bytes 98336 | tf_op jit(solution)/shard_map/ppermute | solution.py:10
  26.0 0.0 collective-permute-start.3
  26.0 5.8 %collective-permute-done.3 = f32[8,3072]{1,0:T(8,128)S(1)} collective-permute-done((f32[8,3072]{1,0:T(8,128)S(1)}, f32[8,3072]{1,0:T(8,128)S(1)}, u32[]{:S(2)}, u32[]{:S(2)}) %collective-permute-start.3) | collective-permute-done | bytes 98336 | tf_op jit(solution)/shard_map/ppermute | solution.py:10
  31.8 0.0 collective-permute-start.4
  31.8 5.8 %collective-permute-done.4 = f32[8,3072]{1,0:T(8,128)S(1)} collective-permute-done((f32[8,3072]{1,0:T(8,128)S(1)}, f32[8,3072]{1,0:T(8,128)S(1)}, u32[]{:S(2)}, u32[]{:S(2)}) %collective-permute-start.4) | collective-permute-done | bytes 98336 | tf_op jit(solution)/shard_map/ppermute | solution.py:10
  37.7 0.0 collective-permute-start.5
  37.7 5.8 %collective-permute-done.5 = f32[8,3072]{1,0:T(8,128)S(1)} collective-permute-done((f32[8,3072]{1,0:T(8,128)S(1)}, f32[8,3072]{1,0:T(8,128)S(1)}, u32[]{:S(2)}, u32[]{:S(2)}) %collective-permute-start.5) | collective-permute-done | bytes 98336 | tf_op jit(solution)/shard_map/ppermute | solution.py:10
  43.5 0.0 collective-permute-start.6
  43.5 5.8 %collective-permute-done.6 = f32[8,3072]{1,0:T(8,128)S(1)} collective-permute-done((f32[8,3072]{1,0:T(8,128)S(1)}, f32[8,3072]{1,0:T(8,128)S(1)}, u32[]{:S(2)}, u32[]{:S(2)}) %collective-permute-start.6) | collective-permute-done | bytes 98336 | tf_op jit(solution)/shard_map/ppermute | solution.py:10
  49.5 0.9 constant_dynamic-update-slice_fusion.8
  50.5 0.0 copy-done
  50.5 9.2 %convolution_bitcast_fusion = f32[640,64]{1,0:T(8,128)} fusion(f32[640,3072]{1,0:T(8,128)} %param.4, f32[128,3072]{1,0:T(8,128)S(1)} %constant_dynamic-update-slice_fusion, s32[]{:T(128)S(6)} %select_n.17), kind=kOutput, calls=%fused_computation | convolution fusion | flops 1509949440 | bytes 8814596
  59.7 0.0 reduce-scatter.7.cloned.1.call-update
  59.7 0.0 reduce-scatter.5.cloned.1.call-start
  59.8 23.3 %reduce-scatter.7.cloned.1.call-done = f32[160,64]{1,0:T(8,128)} async-done(((f32[640,64]{1,0:T(8,128)}), f32[160,64]{1,0:T(8,128)}) %reduce-scatter.7.cloned.1.call-update) | async-done | bytes 40976
  83.1 1.0 copy.8
  84.1 1.0 divide_bitcast_fusion
  85.1 9.5 %all-gather = f32[4,160,64]{1,2,0:T(8,128)S(1)} all-gather(f32[1,160,64]{1,2,0:T(8,128)S(1)} %divide_bitcast_fusion), channel_id=1, replica_groups=mesh['row'=8,'aux'=4] {'aux'}, dimensions={0}, use_global_device_ids=true | all-gather | bytes 204800 | tf_op jit(solution)/shard_map/all_gather | solution.py:25
  94.6 0.2 copy.6
  94.7 0.2 reshape.5
  94.9 8.9 %fusion.5 = f32[64,3072]{1,0:T(8,128)} fusion(f32[640,64]{0,1:T(8,128)S(1)} %reshape.5, f32[640,3072]{1,0:T(8,128)} %param.4), kind=kOutput, calls=%fused_computation.23 | convolution fusion | flops 1509949440 | bytes 8814592 | tf_op jit(solution)/shard_map/dot_general | solution.py:34
  103.8 0.0 reduce-scatter.5.cloned.1.call-update
  103.9 8.5 %fusion = f32[640,3072]{1,0:T(8,128)} fusion(f32[640,64]{0,1:T(8,128)S(1)} %reshape.5, f32[128,3072]{1,0:T(8,128)S(1)} %constant_dynamic-update-slice_fusion, s32[]{:T(128)S(6)} %select_n.17), kind=kOutput, calls=%fused_computation.1 | convolution fusion | flops 1509949440 | bytes 8814596 | tf_op jit(solution)/shard_map/dot_general | solution.py:26
  112.3 23.6 %reduce-scatter.5.cloned.1.call-done = f32[8,3072]{1,0:T(8,128)} async-done(((f32[64,3072]{1,0:T(8,128)}), f32[8,3072]{1,0:T(8,128)}) %reduce-scatter.5.cloned.1.call-update) | async-done | bytes 98320 | tf_op jit(solution)/shard_map/reduce_scatter | solution.py:33
  (15 shorter events, 0.1 us)
Async XLA Ops:
  7.2 43.3 %copy-start = (f32[8,3072]{1,0:T(8,128)S(1)}, f32[8,3072]{1,0:T(8,128)}, u32[]{:S(2)}) copy-start(f32[8,3072]{1,0:T(8,128)} %param.3) | copy-start | bytes 294916
  7.2 76.0 %reduce-scatter.7.cloned.1.call-start = ((), (), s32[]{:S(2)}) async-start(), calls=%async_computation.3 | async-start | bytes 409600
  7.2 7.1 %collective-permute-start = (f32[8,3072]{1,0:T(8,128)}, f32[8,3072]{1,0:T(8,128)S(1)}, u32[]{:S(2)}, u32[]{:S(2)}) collective-permute-start(f32[8,3072]{1,0:T(8,128)} %param.3), channel_id=1, source_target_pairs={{0,4},{4,8},{8,12},{12,16},{16,20},{20,24},{24,28},{28,0},{1,5},{5... | collective-permute-start | bytes 294920 | tf_op jit(solution)/shard_map/ppermute | solution.py:10
  14.3 5.8 %collective-permute-start.1 = (f32[8,3072]{1,0:T(8,128)S(1)}, f32[8,3072]{1,0:T(8,128)S(1)}, u32[]{:S(2)}, u32[]{:S(2)}) collective-permute-start(f32[8,3072]{1,0:T(8,128)S(1)} %collective-permute-done), channel_id=1, source_target_pairs={{0,4},{4,8},{8,12},{12,16},{16,20},{20,24},{24,28},{28,0},{1,5},{5... | collective-permute-start | bytes 294920 | tf_op jit(solution)/shard_map/ppermute | solution.py:10
  20.1 5.8 %collective-permute-start.2 = (f32[8,3072]{1,0:T(8,128)S(1)}, f32[8,3072]{1,0:T(8,128)S(1)}, u32[]{:S(2)}, u32[]{:S(2)}) collective-permute-start(f32[8,3072]{1,0:T(8,128)S(1)} %collective-permute-done.1), channel_id=1, source_target_pairs={{0,4},{4,8},{8,12},{12,16},{16,20},{20,24},{24,28},{28,0},{1,5},{5... | collective-permute-start | bytes 294920 | tf_op jit(solution)/shard_map/ppermute | solution.py:10
  26.0 5.8 %collective-permute-start.3 = (f32[8,3072]{1,0:T(8,128)S(1)}, f32[8,3072]{1,0:T(8,128)S(1)}, u32[]{:S(2)}, u32[]{:S(2)}) collective-permute-start(f32[8,3072]{1,0:T(8,128)S(1)} %collective-permute-done.2), channel_id=1, source_target_pairs={{0,4},{4,8},{8,12},{12,16},{16,20},{20,24},{24,28},{28,0},{1,5},{5... | collective-permute-start | bytes 294920 | tf_op jit(solution)/shard_map/ppermute | solution.py:10
  31.8 5.8 %collective-permute-start.4 = (f32[8,3072]{1,0:T(8,128)S(1)}, f32[8,3072]{1,0:T(8,128)S(1)}, u32[]{:S(2)}, u32[]{:S(2)}) collective-permute-start(f32[8,3072]{1,0:T(8,128)S(1)} %collective-permute-done.3), channel_id=1, source_target_pairs={{0,4},{4,8},{8,12},{12,16},{16,20},{20,24},{24,28},{28,0},{1,5},{5... | collective-permute-start | bytes 294920 | tf_op jit(solution)/shard_map/ppermute | solution.py:10
  37.7 5.8 %collective-permute-start.5 = (f32[8,3072]{1,0:T(8,128)S(1)}, f32[8,3072]{1,0:T(8,128)S(1)}, u32[]{:S(2)}, u32[]{:S(2)}) collective-permute-start(f32[8,3072]{1,0:T(8,128)S(1)} %collective-permute-done.4), channel_id=1, source_target_pairs={{0,4},{4,8},{8,12},{12,16},{16,20},{20,24},{24,28},{28,0},{1,5},{5... | collective-permute-start | bytes 294920 | tf_op jit(solution)/shard_map/ppermute | solution.py:10
  43.5 5.8 %collective-permute-start.6 = (f32[8,3072]{1,0:T(8,128)S(1)}, f32[8,3072]{1,0:T(8,128)S(1)}, u32[]{:S(2)}, u32[]{:S(2)}) collective-permute-start(f32[8,3072]{1,0:T(8,128)S(1)} %collective-permute-done.5), channel_id=1, source_target_pairs={{0,4},{4,8},{8,12},{12,16},{16,20},{20,24},{24,28},{28,0},{1,5},{5... | collective-permute-start | bytes 294920 | tf_op jit(solution)/shard_map/ppermute | solution.py:10
  59.7 76.2 %reduce-scatter.5.cloned.1.call-start = ((), (), s32[]{:S(2)}) async-start(), calls=%async_computation.2 | async-start | bytes 884736 | tf_op jit(solution)/shard_map/reduce_scatter | solution.py:33
Sparse Core Ops, SparseCore 0:
  59.9 23.2 reduce-scatter.6
  104.0 31.9 reduce-scatter.4
